TPU v7x, 32 devices: a whole 2x2x4 slice. The times are simulated.
32 devices in a mesh: group: 2 (over y), row: 4 (over z), src: 4 (over x, core).
Axes of the slice: x: 2, y: 2, z: 4, core: 2. Of those that a mesh axis runs over, the one named last changes fastest.
Arguments:
- right_side: bfloat16 [5120, 1536], P(('group', 'row'), 'src'), parts along dimension 0, may hold values from -6 to 6
- factor: bfloat16 [5120, 2048], P(('group', 'row')), parts along dimension 0, may hold values from -0.1875 to 0.1875
- pattern: int32 [40, 16], P(('group', 'row')), parts along dimension 0, may hold values 0 or 1
- inverses: bfloat16 [8, 512, 512], P('group', 'src'), parts along dimension 0, may hold values from -4 to 4
- owners: int32 [8], P('group'), parts along dimension 0, may hold values from 0 to 3, as said below
- offsets: int32 [8], P('group'), parts along dimension 0, may hold values from 0 to 1
Outputs:
- solved: bfloat16 [4096, 1536], P(('group', 'row'), 'src'), parts along dimension 0
- updated: bfloat16 [5120, 1536], P(('group', 'row'), 'src'), parts along dimension 0
There are 2 independent parts, one for each index of `group`. A program takes and returns all parts, laid end to end along the dimension named above; each array names one. Nothing has to cross between parts.
Inputs may be any that keep to these rules, and one draw needn't show every extreme that they name: The 4 owners are different row indices, and the first and the last row index are always among them.
All inputs are finite; a program needn't handle non-finite values. No bound on the sum of `pattern` on one device may be relied on, other than what follows from the above.
Results may differ from a plain program's by a relative error of at most 0.0057.
Values may be sent and summed in bfloat16 or wider, within the bound.
A program may use at most 64 MiB of HBM per device.

v0:
```python
import functools

import jax
import jax.numpy as jnp
from jax import lax
from jax.experimental import pallas as pl
from jax.experimental.pallas import tpu as pltpu
from jax.sharding import PartitionSpec as P

BLK = 128
PIECES = 4
AHEAD = 4
NEAR, FAR = 0, 1
MESH = pl.DeviceIdType.MESH


def kernel(
    n_row, n_src,
    pattern_in, owners_in, offsets_in, rhs_in, factor, inverses_in, solved, updated,
    pattern, owners, offsets, rhs, inverses,
    panel, whole, running, cand, recv, out, xs,
    other, first, blocks, block,
    load_sem, panel_sem, inv_send, inv_recv, blk_send, blk_recv, send_sem, recv_sem,
):
    sn, rows, snr = panel.shape
    chunks = running.shape[0]
    part = snr // PIECES
    z = lax.axis_index("row")
    s = lax.axis_index("src")
    low = z < n_row // 2
    toward = jnp.where(low, 1, -1)
    far_dev = z + toward
    near_dev = z - toward
    at_end = (z == 0) | (z == n_row - 1)
    inner = jnp.logical_not(at_end)
    crossing = (z == n_row // 2 - 1) | (z == n_row // 2)
    far_slot = jnp.where(crossing, FAR, NEAR)

    small = [
        pltpu.make_async_copy(source, target, load_sem.at[i])
        for i, (source, target) in enumerate((
            (owners_in, owners), (offsets_in, offsets), (pattern_in, pattern),
            (inverses_in, inverses), (rhs_in, rhs),
        ))
    ]
    for load in small:
        load.start()
    loads = [
        pltpu.make_async_copy(factor.at[:, pl.ds(k * snr, snr)], panel.at[k], panel_sem.at[k])
        for k in range(sn)
    ]
    for load in loads:
        load.start()

    barrier = pltpu.get_barrier_semaphore()
    pl.semaphore_signal(barrier, inc=1, device_id={"row": far_dev}, device_id_type=MESH)

    @pl.when(inner)
    def _():
        pl.semaphore_signal(barrier, inc=1, device_id={"row": near_dev}, device_id_type=MESH)

    for d in range(1, n_src):
        pl.semaphore_signal(
            barrier, inc=1, device_id={"src": lax.rem(s + d, n_src)}, device_id_type=MESH
        )

    for load in small:
        load.wait()
    mine = jnp.int32(sn)
    shift = jnp.int32(0)
    for k in range(sn):
        held = owners[k] == z
        mine = jnp.where(held, k, mine)
        shift = jnp.where(held, offsets[k], shift)
    own_rows = inverses[0]
    for k in range(1, sn):
        own_rows = jnp.where(mine == k, inverses[k], own_rows)
    whole[s] = own_rows
    for c in range(chunks):
        running[c] = rhs[:, c * BLK : (c + 1) * BLK].astype(jnp.float32)

    pl.semaphore_wait(barrier, jnp.where(at_end, n_src, n_src + 1))

    def inverse_copy(d, which):
        return pltpu.make_async_remote_copy(
            src_ref=inverses.at[1] if which else whole.at[s],
            dst_ref=other.at[s] if which else whole.at[s],
            send_sem=inv_send.at[which, d],
            recv_sem=inv_recv.at[which, s],
            device_id={"src": lax.rem(s + d, n_src)},
            device_id_type=MESH,
        )

    def inverse_arrival(d, which):
        source = lax.rem(s + n_src - d, n_src)
        held = other if which else whole
        return pltpu.make_async_remote_copy(
            src_ref=held.at[source],
            dst_ref=held.at[source],
            send_sem=inv_send.at[which, d],
            recv_sem=inv_recv.at[which, source],
            device_id={"src": source},
            device_id_type=MESH,
        )

    n_blk = snr // BLK
    b = lax.rem(s, n_blk)

    def block_copy(d):
        return pltpu.make_async_remote_copy(
            src_ref=blocks.at[b],
            dst_ref=blocks.at[b],
            send_sem=blk_send.at[d],
            recv_sem=blk_recv.at[b],
            device_id={"src": s - b + lax.rem(b + d, n_blk)},
            device_id_type=MESH,
        )

    def block_arrival(d):
        source = lax.rem(b + n_blk - d, n_blk)
        return pltpu.make_async_remote_copy(
            src_ref=blocks.at[source],
            dst_ref=blocks.at[source],
            send_sem=blk_send.at[d],
            recv_sem=blk_recv.at[source],
            device_id={"src": s - b + source},
            device_id_type=MESH,
        )

    for d in range(1, n_src):
        inverse_copy(d, 0).start()
    for d in range(1, n_src):
        inverse_copy(d, 1).start()
    other[s] = inverses[1]

    def mask(k):
        loads[k].wait()
        for t in range(rows // BLK):
            inside = (t >= shift) & (t < shift + snr // BLK)
            rank = jnp.where(inside, mine, sn)
            for j in range(snr // BLK):
                keep = (pattern[t, k * (snr // BLK) + j] > 0) & (rank > k)
                tile = panel[k, t * BLK : (t + 1) * BLK, j * BLK : (j + 1) * BLK]
                panel[k, t * BLK : (t + 1) * BLK, j * BLK : (j + 1) * BLK] = jnp.where(
                    keep, tile, jnp.zeros_like(tile)
                )

    def message(way, k, c, p):
        span = pl.ds(p * part, part)
        return pltpu.make_async_remote_copy(
            src_ref=out.at[way, k, c, span],
            dst_ref=recv.at[far_slot if way == FAR else FAR, k, c, span],
            send_sem=send_sem.at[way, k, c, p],
            recv_sem=recv_sem.at[far_slot if way == FAR else FAR, k, c, p],
            device_id={"row": far_dev if way == FAR else near_dev},
            device_id_type=MESH,
        )

    def arrival(way, k, c, p):
        span = pl.ds(p * part, part)
        return pltpu.make_async_remote_copy(
            src_ref=out.at[way, k, c, span],
            dst_ref=recv.at[way, k, c, span],
            send_sem=send_sem.at[way, k, c, p],
            recv_sem=recv_sem.at[way, k, c, p],
            device_id={"row": far_dev if way == FAR else near_dev},
            device_id_type=MESH,
        )

    def offer(k, c, value):
        cand[k, c] = value

        @pl.when(at_end)
        def _():
            out[FAR, k, c] = value
            for p in range(PIECES):
                message(FAR, k, c, p).start()

    def segment_of(read):
        found = read(0)
        for t in range(1, (rows - snr) // BLK + 1):
            found = jnp.where(shift == t, read(t * BLK), found)
        return found

    def own_segment(c):
        return segment_of(lambda t: running[c, t : t + snr]).astype(jnp.bfloat16)

    def candidate(k, c):
        offer(k, c, jnp.dot(
            whole[...].reshape(snr, snr), own_segment(c), preferred_element_type=jnp.float32
        ).astype(jnp.bfloat16))

    def node(k):
        if isinstance(k, int):
            return (1, 0)[k] if k < 2 else 1 if k == sn else k
        return k

    def forward(k, c, p, came, way):
        arrival(came, k, c, p).wait_recv()
        span = pl.ds(p * part, part)
        out[way, k, c, span] = jnp.where(
            mine == node(k), cand[k, c, span], recv[came, k, c, span]
        )
        message(way, k, c, p).start()

    opening = [(sn, 0)] + [(k, c) for c in range(chunks) for k in (0, 1)]

    def near_forward(k, place):
        c, p = divmod(place, PIECES)
        if isinstance(k, int):
            later = opening.index((k, 0)) + c if k == sn else c
            k, c = opening[later] if later < len(opening) else (2, later - len(opening))
            forward(k, c, p, NEAR, FAR)
        elif c < chunks:
            forward(k, c, p, NEAR, FAR)
        else:
            @pl.when(k + 1 < sn)
            def _():
                forward(k + 1, c - chunks, p, NEAR, FAR)

    def exchange(k, c):
        @pl.when(inner)
        def _():
            for p in range(PIECES):
                base = opening.index((k, c)) if isinstance(k, int) else c
                near_forward(sn if isinstance(k, int) else k, base * PIECES + p + AHEAD)
                forward(k, c, p, FAR, NEAR)

        @pl.when(at_end)
        def _():
            for p in range(PIECES):
                arrival(FAR, k, c, p).wait_recv()

    def pick(k, c):
        owner = owners[node(k)]
        from_near = jnp.where(low, z - owner, owner - z) > 0
        return jnp.where(
            mine == node(k),
            cand[k, c],
            jnp.where(from_near, recv[NEAR, k, c], recv[FAR, k, c]),
        )

    def update(k, c, x):
        begin = k * snr if isinstance(k, int) else pl.multiple_of(k * snr, snr)
        xs[c, pl.ds(begin, snr)] = x
        running[c] = running[c] - jnp.dot(panel[k], x, preferred_element_type=jnp.float32)

    @pl.when(at_end)
    def _():
        recv[NEAR] = jnp.zeros_like(recv[NEAR])

    mask(0)
    stored = segment_of(lambda t: panel[0, t : t + snr, :BLK])
    for j in range(1, n_blk):
        column = segment_of(lambda t: panel[0, t : t + snr, j * BLK : (j + 1) * BLK])
        stored = jnp.where(b == j, column, stored)
    offer(sn, 0, stored)
    offer(0, 0, own_segment(0))
    for d in range(1, n_src):
        inverse_arrival(d, 0).wait_recv()
    for c in range(chunks):
        if c > 0:
            offer(0, c, own_segment(c))
        candidate(1, c)

    @pl.when(inner)
    def _():
        for place in range(AHEAD):
            near_forward(sn, place)

    exchange(sn, 0)
    blocks[b] = pick(sn, 0)
    for d in range(1, n_blk):
        block_copy(d).start()
    for k in range(1, sn):
        mask(k)
    for c in range(chunks):
        exchange(0, c)
        first[c] = pick(0, c)
        exchange(1, c)
        if c == 0:
            for d in range(1, n_src):
                inverse_arrival(d, 1).wait_recv()
            for d in range(1, n_blk):
                block_arrival(d).wait_recv()
            for j in range(n_blk):
                block[:, j * BLK : (j + 1) * BLK] = blocks[j]
        x = pick(1, c)
        segment = first[c].astype(jnp.float32) - jnp.dot(
            block[...], x, preferred_element_type=jnp.float32
        )
        update(0, c, x)
        update(1, c, jnp.dot(
            other[...].reshape(snr, snr),
            segment.astype(jnp.bfloat16),
            preferred_element_type=jnp.float32,
        ).astype(jnp.bfloat16))
        candidate(2, c)

    def step(k, carry):
        for c in range(chunks):
            exchange(k, c)
            update(k, c, pick(k, c))

            @pl.when(k + 1 < sn)
            def _():
                candidate(k + 1, c)
        return carry

    lax.fori_loop(2, sn, step, 0)

    kept = solved.shape[0]
    begin = pl.multiple_of(z * kept, kept)
    for c in range(chunks):
        updated[:, c * BLK : (c + 1) * BLK] = running[c].astype(updated.dtype)
        solved[:, c * BLK : (c + 1) * BLK] = xs[c, pl.ds(begin, kept)]

    for d in range(1, n_src):
        inverse_copy(d, 0).wait_send()
        inverse_copy(d, 1).wait_send()
    for d in range(1, n_blk):
        block_copy(d).wait_send()
    for p in range(PIECES):
        message(FAR, sn, 0, p).wait_send()

        @pl.when(inner)
        def _():
            message(NEAR, sn, 0, p).wait_send()

    def drain(k, carry):
        for c in range(chunks):
            for p in range(PIECES):
                message(FAR, k, c, p).wait_send()

                @pl.when(inner)
                def _():
                    message(NEAR, k, c, p).wait_send()
        return carry

    lax.fori_loop(0, sn, drain, 0)


def solution(mesh):
    n_row, n_src = mesh.shape["row"], mesh.shape["src"]

    def on_device(right_side, factor, pattern, inverses, owners, offsets):
        rows, cols = right_side.shape
        sn, inv_rows, snr = inverses.shape
        chunks = cols // BLK
        vmem = pl.BlockSpec(memory_space=pltpu.VMEM)
        hbm = pl.BlockSpec(memory_space=pltpu.HBM)
        kept = sn * snr // n_row
        return pl.pallas_call(
            functools.partial(kernel, n_row, n_src),
            out_shape=(
                jax.ShapeDtypeStruct((kept, cols), jnp.bfloat16),
                jax.ShapeDtypeStruct((rows, cols), jnp.bfloat16),
            ),
            in_specs=[hbm] * 6,
            out_specs=(vmem, vmem),
            scratch_shapes=[
                pltpu.SMEM(pattern.shape, jnp.int32),
                pltpu.SMEM(owners.shape, jnp.int32),
                pltpu.SMEM(offsets.shape, jnp.int32),
                pltpu.VMEM(right_side.shape, jnp.bfloat16),
                pltpu.VMEM(inverses.shape, jnp.bfloat16),
                pltpu.VMEM((sn, rows, snr), jnp.bfloat16),
                pltpu.VMEM((n_src, inv_rows, snr), jnp.bfloat16),
                pltpu.VMEM((chunks, rows, BLK), jnp.float32),
                pltpu.VMEM((sn + 1, chunks, snr, BLK), jnp.bfloat16),
                pltpu.VMEM((2, sn + 1, chunks, snr, BLK), jnp.bfloat16),
                pltpu.VMEM((2, sn + 1, chunks, snr, BLK), jnp.bfloat16),
                pltpu.VMEM((chunks, sn * snr, BLK), jnp.bfloat16),
                pltpu.VMEM((n_src, inv_rows, snr), jnp.bfloat16),
                pltpu.VMEM((chunks, snr, BLK), jnp.bfloat16),
                pltpu.VMEM((snr // BLK, snr, BLK), jnp.bfloat16),
                pltpu.VMEM((snr, snr), jnp.bfloat16),
                pltpu.SemaphoreType.DMA((5,)),
                pltpu.SemaphoreType.DMA((sn,)),
                pltpu.SemaphoreType.DMA((2, n_src)),
                pltpu.SemaphoreType.DMA((2, n_src)),
                pltpu.SemaphoreType.DMA((snr // BLK,)),
                pltpu.SemaphoreType.DMA((snr // BLK,)),
                pltpu.SemaphoreType.DMA((2, sn + 1, chunks, PIECES)),
                pltpu.SemaphoreType.DMA((2, sn + 1, chunks, PIECES)),
            ],
            compiler_params=pltpu.CompilerParams(
                collective_id=0, has_side_effects=True, vmem_limit_bytes=48 * 1024 * 1024
            ),
        )(pattern, owners, offsets, right_side, factor, inverses)

    return jax.shard_map(
        on_device,
        mesh=mesh,
        in_specs=(
            P(("group", "row"), "src"),
            P(("group", "row"), None),
            P(("group", "row"), None),
            P("group", "src", None),
            P("group"),
            P("group"),
        ),
        out_specs=(P(("group", "row"), "src"), P(("group", "row"), "src")),
        check_vma=False,
    )
```

profile of v0, /device:TPU:0, one launch (start us, length us, event | category | flops | bytes accessed | tf_op | source)
XLA Modules:
  0.0 72.1 jit_solution(17221300208919178054)
XLA Ops:
  0.6 0.0 copy-start
  0.6 1.7 %copy-done = bf16[640,2048]{1,0:T(8,128)(2,1)S(1)} copy-done((bf16[640,2048]{1,0:T(8,128)(2,1)S(1)}, bf16[640,2048]{1,0:T(8,128)(2,1)}, u32[]{:S(2)}) %copy-start) | copy-done | bytes 2621464
  2.4 0.0 copy-start.1
  2.4 1.0 %copy-done.1 = bf16[4,128,512]{2,1,0:T(8,128)(2,1)S(1)} copy-done((bf16[4,128,512]{2,1,0:T(8,128)(2,1)S(1)}, bf16[4,128,512]{2,1,0:T(8,128)(2,1)}, u32[]{:S(2)}) %copy-start.1) | copy-done | bytes 524312
  3.4 0.0 copy-start.2
  3.4 1.0 %copy-done.2 = bf16[640,384]{1,0:T(8,128)(2,1)S(1)} copy-done((bf16[640,384]{1,0:T(8,128)(2,1)S(1)}, bf16[640,384]{1,0:T(8,128)(2,1)}, u32[]{:S(2)}) %copy-start.2) | copy-done | bytes 491544
  4.4 0.0 copy-start.3
  4.4 0.7 copy-done.3
  5.1 0.0 copy-start.4
  5.1 0.7 copy-done.4
  5.8 0.0 copy-start.5
  5.8 0.7 copy-done.5
  6.4 64.1 %shard_map.77 = (bf16[512,384]{1,0:T(8,128)(2,1)S(1)}, bf16[640,384]{1,0:T(8,128)(2,1)S(1)}) custom-call(s32[5,16]{1,0:T(8,128)S(1)} %copy-done.3, s32[4]{0:T(128)S(1)} %copy-done.4, s32[4]{0:T(128)S(1)} %copy-done.5, bf16[640,384]{1,0:T(8,128)(2,1)S(1)} %copy-done.2, bf16[640,2048]{1,0:T(8,128)(2,1)S(1)} %copy-done, bf16[4,128,512]{2,1,0:T(8,128)(2,1)S(1)} %copy-done.1), custom_call_target="tpu_custom_call" | custom-call | tf_op jit(solution)/shard_map/pallas_call | solution.py:353
  70.5 0.7 %copy.10 = bf16[512,384]{1,0:T(8,128)(2,1)} copy(bf16[512,384]{1,0:T(8,128)(2,1)S(1)} %get-tuple-element.4) | data formatting | bytes 786432
  71.3 0.8 %copy.11 = bf16[640,384]{1,0:T(8,128)(2,1)} copy(bf16[640,384]{1,0:T(8,128)(2,1)S(1)} %get-tuple-element.5) | data formatting | bytes 983040
Async XLA Ops:
  0.6 1.7 %copy-start = (bf16[640,2048]{1,0:T(8,128)(2,1)S(1)}, bf16[640,2048]{1,0:T(8,128)(2,1)}, u32[]{:S(2)}) copy-start(bf16[640,2048]{1,0:T(8,128)(2,1)} %factor.1) | copy-start | bytes 7864324
  2.4 1.0 %copy-start.1 = (bf16[4,128,512]{2,1,0:T(8,128)(2,1)S(1)}, bf16[4,128,512]{2,1,0:T(8,128)(2,1)}, u32[]{:S(2)}) copy-start(bf16[4,128,512]{2,1,0:T(8,128)(2,1)} %inverses_in.1) | copy-start | bytes 1572868
  3.4 1.0 %copy-start.2 = (bf16[640,384]{1,0:T(8,128)(2,1)S(1)}, bf16[640,384]{1,0:T(8,128)(2,1)}, u32[]{:S(2)}) copy-start(bf16[640,384]{1,0:T(8,128)(2,1)} %rhs_in.1) | copy-start | bytes 1474564
  4.4 0.7 copy-start.3
  5.1 0.7 copy-start.4
  5.8 0.7 copy-start.5
where the time goes:
time: 72.3 us; the launch traced here: 72.1 us
  Pallas kernels  64.1 us (89%)
  local copies, waits for them, and re-layouts  7.33 us (10%)
    pallas_call x1, Pallas kernels, on_device(): pl.pallas_call(functools.partial(kernel, n_row, n_src), out_shape=(jax.Sh...  64.1 us
    unnamed x14, local copies, waits for them, and re-layouts  7.33 us

commit v1 on v0

--- a/solution.py
+++ b/solution.py
@@ -14,7 +14,7 @@
 MESH = pl.DeviceIdType.MESH
 
 
-def kernel(
+def chain_kernel(
     n_row, n_src,
     pattern_in, owners_in, offsets_in, rhs_in, factor, inverses_in, solved, updated,
     pattern, owners, offsets, rhs, inverses,
@@ -340,6 +340,364 @@
     lax.fori_loop(0, sn, drain, 0)
 
 
+def pair_kernel(
+    n_row, n_src,
+    pattern_in, owners_in, offsets_in, rhs_in, factor, inverses_in, solved, updated,
+    pattern, owners, offsets, rhs, panel, invs, running, xs,
+    own, near, far_own, far_near, down_units, picked, blocks, lower,
+    load_sem, panel_sem, inv_load, inv_send, inv_recv, blk_send, blk_recv,
+    own_send, near_recv, far_own_recv, relay_send, far_near_recv, down_send, down_recv,
+):
+    chunks, rows, _ = running.shape
+    snr = own.shape[1]
+    sn = owners.shape[0]
+    n_blk = snr // BLK
+    part = snr // PIECES
+    fac = chunks
+    z = lax.axis_index("row")
+    s = lax.axis_index("src")
+    low = z < n_row // 2
+    toward = jnp.where(low, 1, -1)
+    far_dev = z + toward
+    near_dev = z - toward
+    at_end = (z == 0) | (z == n_row - 1)
+    inner = jnp.logical_not(at_end)
+
+    small = [
+        pltpu.make_async_copy(source, target, load_sem.at[i])
+        for i, (source, target) in enumerate((
+            (owners_in, owners), (offsets_in, offsets), (rhs_in, rhs), (pattern_in, pattern),
+        ))
+    ]
+    for load in small:
+        load.start()
+    inv_loads = [
+        pltpu.make_async_copy(inverses_in.at[k], invs.at[k, s], inv_load.at[k]) for k in range(sn)
+    ]
+    loads = [
+        pltpu.make_async_copy(factor.at[:, pl.ds(k * snr, snr)], panel.at[:, pl.ds(k * snr, snr)], panel_sem.at[k])
+        for k in range(sn)
+    ]
+    for k in (0, 1):
+        inv_loads[k].start()
+    for k in (0, 2, 1, 3):
+        loads[k].start()
+    for k in (2, 3):
+        inv_loads[k].start()
+
+    barrier = pltpu.get_barrier_semaphore()
+    pl.semaphore_signal(barrier, inc=1, device_id={"row": far_dev}, device_id_type=MESH)
+
+    @pl.when(inner)
+    def _():
+        pl.semaphore_signal(barrier, inc=1, device_id={"row": near_dev}, device_id_type=MESH)
+
+    for d in range(1, n_src):
+        pl.semaphore_signal(
+            barrier, inc=1, device_id={"src": lax.rem(s + d, n_src)}, device_id_type=MESH
+        )
+
+    for load in small[:3]:
+        load.wait()
+    mine = jnp.int32(sn)
+    shift = jnp.int32(0)
+    for k in range(sn):
+        held = owners[k] == z
+        mine = jnp.where(held, k, mine)
+        shift = jnp.where(held, offsets[k], shift)
+
+    def segment_of(read):
+        found = read(0)
+        for t in range(1, (rows - snr) // BLK + 1):
+            found = jnp.where(shift == t, read(t * BLK), found)
+        return found
+
+    def raw(c):
+        own[c] = segment_of(lambda t: rhs[t : t + snr, c * BLK : (c + 1) * BLK])
+
+    def span(p):
+        return pl.ds(p * part, part)
+
+    def own_up(u, p):
+        return pltpu.make_async_remote_copy(
+            src_ref=own.at[u, span(p)], dst_ref=near.at[u, span(p)],
+            send_sem=own_send.at[u, p], recv_sem=near_recv.at[u, p],
+            device_id={"row": far_dev}, device_id_type=MESH,
+        )
+
+    def own_across(u, p):
+        return pltpu.make_async_remote_copy(
+            src_ref=own.at[u, span(p)], dst_ref=far_own.at[u, span(p)],
+            send_sem=own_send.at[u, p], recv_sem=far_own_recv.at[u, p],
+            device_id={"row": far_dev}, device_id_type=MESH,
+        )
+
+    def near_across(u, p):
+        return pltpu.make_async_remote_copy(
+            src_ref=near.at[u, span(p)], dst_ref=far_near.at[u, span(p)],
+            send_sem=relay_send.at[u, p], recv_sem=far_near_recv.at[u, p],
+            device_id={"row": far_dev}, device_id_type=MESH,
+        )
+
+    def from_near(u, p):
+        return pltpu.make_async_remote_copy(
+            src_ref=own.at[u, span(p)], dst_ref=near.at[u, span(p)],
+            send_sem=own_send.at[u, p], recv_sem=near_recv.at[u, p],
+            device_id={"row": near_dev}, device_id_type=MESH,
+        )
+
+    def down(u, q, p, to):
+        return pltpu.make_async_remote_copy(
+            src_ref=down_units.at[u, q, span(p)], dst_ref=down_units.at[u, q, span(p)],
+            send_sem=down_send.at[u, q, p], recv_sem=down_recv.at[u, q, p],
+            device_id={"row": to}, device_id_type=MESH,
+        )
+
+    def post_inner(u):
+        @pl.when(inner)
+        def _():
+            for p in range(PIECES):
+                own_across(u, p).start()
+
+    def post_end(u):
+        @pl.when(at_end)
+        def _():
+            for p in range(PIECES):
+                own_up(u, p).start()
+
+    def relay(u):
+        @pl.when(inner)
+        def _():
+            for p in range(PIECES):
+                from_near(u, p).wait_recv()
+                near_across(u, p).start()
+
+    def nodes(u):
+        return (0, 1) if u < chunks else (1, 3) if u == fac else (2, 3)
+
+    def holds(device, u):
+        first, second = nodes(u)
+        return (owners[first] == device) | (owners[second] == device)
+
+    def down_early(u):
+        @pl.when(inner)
+        def _():
+            use = holds(z, u)
+            for p in range(PIECES):
+                own_across(u, p).wait_recv()
+                down_units[u, 0, span(p)] = jnp.where(use, own[u, span(p)], far_own[u, span(p)])
+                down(u, 0, p, near_dev).start()
+
+        @pl.when(at_end)
+        def _():
+            for p in range(PIECES):
+                down(u, 0, p, far_dev).wait_recv()
+
+    def down_late(u):
+        @pl.when(inner)
+        def _():
+            use = holds(z + 2 * toward, u)
+            for p in range(PIECES):
+                near_across(u, p).wait_recv()
+                down_units[u, 1, span(p)] = jnp.where(use, far_near[u, span(p)], far_own[u, span(p)])
+                down(u, 1, p, near_dev).start()
+
+        @pl.when(at_end)
+        def _():
+            for p in range(PIECES):
+                down(u, 1, p, far_dev).wait_recv()
+
+    def pick(u):
+        @pl.when(inner)
+        def _():
+            for q, k in enumerate(nodes(u)):
+                picked[q] = jnp.where(
+                    mine == k,
+                    own[u],
+                    jnp.where(
+                        owners[k] == near_dev,
+                        near[u],
+                        jnp.where(owners[k] == far_dev, far_own[u], far_near[u]),
+                    ),
+                )
+
+        @pl.when(at_end)
+        def _():
+            for q, k in enumerate(nodes(u)):
+                first = (owners[k] == far_dev) | (
+                    (owners[k] == z + 2 * toward) & jnp.logical_not(holds(far_dev, u))
+                )
+                picked[q] = jnp.where(
+                    mine == k, own[u], jnp.where(first, down_units[u, 0], down_units[u, 1])
+                )
+
+    def inverse_copy(d, k):
+        return pltpu.make_async_remote_copy(
+            src_ref=invs.at[k, s], dst_ref=invs.at[k, s],
+            send_sem=inv_send.at[k, d], recv_sem=inv_recv.at[k, s],
+            device_id={"src": lax.rem(s + d, n_src)}, device_id_type=MESH,
+        )
+
+    def inverse_arrival(d, k):
+        source = lax.rem(s + n_src - d, n_src)
+        return pltpu.make_async_remote_copy(
+            src_ref=invs.at[k, source], dst_ref=invs.at[k, source],
+            send_sem=inv_send.at[k, d], recv_sem=inv_recv.at[k, source],
+            device_id={"src": source}, device_id_type=MESH,
+        )
+
+    def block_copy(d, q):
+        return pltpu.make_async_remote_copy(
+            src_ref=blocks.at[q, s], dst_ref=blocks.at[q, s],
+            send_sem=blk_send.at[q, d], recv_sem=blk_recv.at[q, s],
+            device_id={"src": lax.rem(s + d, n_src)}, device_id_type=MESH,
+        )
+
+    def block_arrival(d, q):
+        source = lax.rem(s + n_src - d, n_src)
+        return pltpu.make_async_remote_copy(
+            src_ref=blocks.at[q, source], dst_ref=blocks.at[q, source],
+            send_sem=blk_send.at[q, d], recv_sem=blk_recv.at[q, source],
+            device_id={"src": source}, device_id_type=MESH,
+        )
+
+    def mask(k):
+        loads[k].wait()
+        for t in range(rows // BLK):
+            inside = (t >= shift) & (t < shift + n_blk)
+            rank = jnp.where(inside, mine, sn)
+            for j in range(n_blk):
+                keep = (pattern[t, k * n_blk + j] > 0) & (rank > k)
+                at = (slice(t * BLK, (t + 1) * BLK), slice((k * n_blk + j) * BLK, (k * n_blk + j + 1) * BLK))
+                tile = panel[at]
+                panel[at] = jnp.where(keep, tile, jnp.zeros_like(tile))
+
+    def inverse(k, value):
+        return jnp.dot(
+            invs[k].reshape(snr, snr), value, preferred_element_type=jnp.float32
+        ).astype(jnp.bfloat16)
+
+    def gathered(q):
+        for d in range(1, n_src):
+            block_arrival(d, q).wait_recv()
+        for j in range(n_src):
+            lower[q, :, j * BLK : (j + 1) * BLK] = blocks[q, j]
+        for k in (2 * q, 2 * q + 1):
+            for d in range(1, n_src):
+                inverse_arrival(d, k).wait_recv()
+
+    def solve(q, u, c):
+        pick(u)
+        first = inverse(2 * q, picked[0])
+        segment = picked[1].astype(jnp.float32) - jnp.dot(
+            lower[q], first, preferred_element_type=jnp.float32
+        )
+        second = inverse(2 * q + 1, segment.astype(jnp.bfloat16))
+        begin = 2 * q * snr
+        xs[c, begin : begin + snr] = first
+        xs[c, begin + snr : begin + 2 * snr] = second
+        running[c] = running[c] - jnp.dot(
+            panel[:, begin : begin + 2 * snr], xs[c, begin : begin + 2 * snr],
+            preferred_element_type=jnp.float32,
+        )
+
+    def early(c):
+        solve(0, c, c)
+        own[fac + 1 + c] = segment_of(lambda t: running[c, t : t + snr]).astype(jnp.bfloat16)
+        post_inner(fac + 1 + c)
+        post_end(fac + 1 + c)
+
+    kept = solved.shape[0]
+
+    def late(c):
+        solve(1, fac + 1 + c, c)
+        at = slice(c * BLK, (c + 1) * BLK)
+        updated[:, at] = running[c].astype(updated.dtype)
+        solved[:, at] = xs[c, pl.ds(pl.multiple_of(z * kept, kept), kept)]
+
+    raw(0)
+    pl.semaphore_wait(barrier, jnp.where(at_end, n_src, n_src + 1))
+    post_inner(0)
+    for k in (0, 1):
+        inv_loads[k].wait()
+        for d in range(1, n_src):
+            inverse_copy(d, k).start()
+    small[3].wait()
+    mask(0)
+    mask(2)
+    columns = [pl.ds(pl.multiple_of((k * n_blk + s) * BLK, BLK), BLK) for k in (0, 2)]
+    own[fac] = jnp.where(
+        mine == 1,
+        segment_of(lambda t: panel[t : t + snr, columns[0]]),
+        segment_of(lambda t: panel[t : t + snr, columns[1]]),
+    )
+    post_inner(fac)
+    post_end(fac)
+    for c in range(1, chunks):
+        raw(c)
+    for c in range(chunks):
+        post_end(c)
+    mask(1)
+    mask(3)
+    for c in range(chunks):
+        running[c] = rhs[:, c * BLK : (c + 1) * BLK].astype(jnp.float32)
+
+    relay(fac)
+    relay(0)
+    down_early(0)
+    down_early(fac)
+    if chunks > 1:
+        post_inner(1)
+    down_late(fac)
+    pick(fac)
+    for q in range(2):
+        blocks[q, s] = picked[q]
+        for d in range(1, n_src):
+            block_copy(d, q).start()
+    for k in (2, 3):
+        inv_loads[k].wait()
+        for d in range(1, n_src):
+            inverse_copy(d, k).start()
+    for c in range(1, chunks):
+        relay(c)
+        if c + 1 < chunks:
+            post_inner(c + 1)
+        down_late(c - 1)
+        if c + 1 < chunks:
+            down_early(c)
+    gathered(0)
+    for c in range(chunks):
+        if c == chunks - 1:
+            if c > 0:
+                down_early(c)
+                early(c - 1)
+            down_late(c)
+            early(c)
+        elif c < chunks - 2:
+            early(c)
+    for c in range(chunks):
+        relay(fac + 1 + c)
+        down_early(fac + 1 + c)
+    gathered(1)
+    for c in range(chunks):
+        down_late(fac + 1 + c)
+        late(c)
+
+    for u in range(2 * chunks + 1):
+        for p in range(PIECES):
+            own_up(u, p).wait_send()
+
+            @pl.when(inner)
+            def _():
+                near_across(u, p).wait_send()
+                for q in range(2):
+                    down(u, q, p, near_dev).wait_send()
+    for d in range(1, n_src):
+        for k in range(sn):
+            inverse_copy(d, k).wait_send()
+        for q in range(2):
+            block_copy(d, q).wait_send()
+
 def solution(mesh):
     n_row, n_src = mesh.shape["row"], mesh.shape["src"]
 
@@ -350,8 +708,52 @@
         vmem = pl.BlockSpec(memory_space=pltpu.VMEM)
         hbm = pl.BlockSpec(memory_space=pltpu.HBM)
         kept = sn * snr // n_row
+        if n_row == sn == 4 and n_src == snr // BLK:
+            units = 2 * chunks + 1
+            unit = (snr, BLK)
+            pieces = pltpu.SemaphoreType.DMA((units, PIECES))
+            return pl.pallas_call(
+                functools.partial(pair_kernel, n_row, n_src),
+                out_shape=(
+                    jax.ShapeDtypeStruct((kept, cols), jnp.bfloat16),
+                    jax.ShapeDtypeStruct((rows, cols), jnp.bfloat16),
+                ),
+                in_specs=[hbm] * 6,
+                out_specs=(vmem, vmem),
+                scratch_shapes=[
+                    pltpu.SMEM(pattern.shape, jnp.int32),
+                    pltpu.SMEM(owners.shape, jnp.int32),
+                    pltpu.SMEM(offsets.shape, jnp.int32),
+                    pltpu.VMEM(right_side.shape, jnp.bfloat16),
+                    pltpu.VMEM(factor.shape, jnp.bfloat16),
+                    pltpu.VMEM((sn, n_src, inv_rows, snr), jnp.bfloat16),
+                    pltpu.VMEM((chunks, rows, BLK), jnp.float32),
+                    pltpu.VMEM((chunks, sn * snr, BLK), jnp.bfloat16),
+                    pltpu.VMEM((units, *unit), jnp.bfloat16),
+                    pltpu.VMEM((units, *unit), jnp.bfloat16),
+                    pltpu.VMEM((units, *unit), jnp.bfloat16),
+                    pltpu.VMEM((units, *unit), jnp.bfloat16),
+                    pltpu.VMEM((units, 2, *unit), jnp.bfloat16),
+                    pltpu.VMEM((2, *unit), jnp.bfloat16),
+                    pltpu.VMEM((2, n_src, *unit), jnp.bfloat16),
+                    pltpu.VMEM((2, snr, snr), jnp.bfloat16),
+                    pltpu.SemaphoreType.DMA((4,)),
+                    pltpu.SemaphoreType.DMA((sn,)),
+                    pltpu.SemaphoreType.DMA((sn,)),
+                    pltpu.SemaphoreType.DMA((sn, n_src)),
+                    pltpu.SemaphoreType.DMA((sn, n_src)),
+                    pltpu.SemaphoreType.DMA((2, n_src)),
+                    pltpu.SemaphoreType.DMA((2, n_src)),
+                    pieces, pieces, pieces, pieces, pieces,
+                    pltpu.SemaphoreType.DMA((units, 2, PIECES)),
+                    pltpu.SemaphoreType.DMA((units, 2, PIECES)),
+                ],
+                compiler_params=pltpu.CompilerParams(
+                    collective_id=0, has_side_effects=True, vmem_limit_bytes=63 * 1024 * 1024
+                ),
+            )(pattern, owners, offsets, right_side, factor, inverses)
         return pl.pallas_call(
-            functools.partial(kernel, n_row, n_src),
+            functools.partial(chain_kernel, n_row, n_src),
             out_shape=(
                 jax.ShapeDtypeStruct((kept, cols), jnp.bfloat16),
                 jax.ShapeDtypeStruct((rows, cols), jnp.bfloat16),
@@ -385,7 +787,7 @@
                 pltpu.SemaphoreType.DMA((2, sn + 1, chunks, PIECES)),
             ],
             compiler_params=pltpu.CompilerParams(
-                collective_id=0, has_side_effects=True, vmem_limit_bytes=48 * 1024 * 1024
+                collective_id=0, has_side_effects=True, vmem_limit_bytes=63 * 1024 * 1024
             ),
         )(pattern, owners, offsets, right_side, factor, inverses)
 

time: 72.3 us -> 66.6 us (0.921)
  local copies, waits for them, and re-layouts: 7.33 us -> 3.64 us
  Pallas kernels: 64.1 us -> 62.1 us
    unnamed x14 -> x2, local copies, waits for them, and re-layouts: 7.33 us -> 3.64 us
    pallas_call x1, Pallas kernels: 64.1 us -> 62.1 us  [on_device(): pl.pallas_call(functools.partial(pair_kernel, n_row, n_src), out_shape=(j...]
where the time goes in v1:
time: 66.6 us; the launch traced here: 66.3 us
  Pallas kernels  62.1 us (93%)
  local copies, waits for them, and re-layouts  3.64 us (5%)
    pallas_call x1, Pallas kernels, on_device(): pl.pallas_call(functools.partial(pair_kernel, n_row, n_src), out_shape=(j...  62.1 us
    unnamed x2, local copies, waits for them, and re-layouts  3.64 us

profile of v1, /device:TPU:0, one launch (start us, length us, event | category | flops | bytes accessed | tf_op | source)
XLA Modules:
  0.0 66.3 jit_solution(2364390950396097828)
XLA Ops:
  0.6 62.1 %shard_map.77 = (bf16[512,384]{1,0:T(8,128)(2,1)}, bf16[640,384]{1,0:T(8,128)(2,1)}) custom-call(s32[5,16]{1,0:T(8,128)} %pattern_in.1, s32[4]{0:T(128)} %owners_in.1, s32[4]{0:T(128)} %offsets_in.1, bf16[640,384]{1,0:T(8,128)(2,1)} %rhs_in.1, bf16[640,2048]{1,0:T(8,128)(2,1)} %factor.1, bf16[4,128,512]{2,1,0:T(8,128)(2,1)} %inverses_in.1), custom_call_target="tpu_custom_call" | custom-call | tf_op jit(solution)/shard_map/pallas_call | solution.py:715
  62.7 1.8 %copy.10 = bf16[512,384]{1,0:T(8,128)(2,1)} copy(bf16[512,384]{1,0:T(8,128)(2,1)} %get-tuple-element.4) | data formatting | bytes 786432
  64.5 1.9 %copy.11 = bf16[640,384]{1,0:T(8,128)(2,1)} copy(bf16[640,384]{1,0:T(8,128)(2,1)} %get-tuple-element.5) | data formatting | bytes 983040

commit v2 on v1

--- a/solution.py
+++ b/solution.py
@@ -8,7 +8,7 @@
 from jax.sharding import PartitionSpec as P
 
 BLK = 128
-PIECES = 4
+PIECES = 2
 AHEAD = 4
 NEAR, FAR = 0, 1
 MESH = pl.DeviceIdType.MESH
@@ -342,8 +342,8 @@
 
 def pair_kernel(
     n_row, n_src,
-    pattern_in, owners_in, offsets_in, rhs_in, factor, inverses_in, solved, updated,
-    pattern, owners, offsets, rhs, panel, invs, running, xs,
+    pattern, owners, offsets, rhs_in, factor, inverses_in, solved, updated,
+    rhs, panel, invs, running, xs,
     own, near, far_own, far_near, down_units, picked, blocks, lower,
     load_sem, panel_sem, inv_load, inv_send, inv_recv, blk_send, blk_recv,
     own_send, near_recv, far_own_recv, relay_send, far_near_recv, down_send, down_recv,
@@ -365,9 +365,7 @@
 
     small = [
         pltpu.make_async_copy(source, target, load_sem.at[i])
-        for i, (source, target) in enumerate((
-            (owners_in, owners), (offsets_in, offsets), (rhs_in, rhs), (pattern_in, pattern),
-        ))
+        for i, (source, target) in enumerate(((rhs_in, rhs),))
     ]
     for load in small:
         load.start()
@@ -397,7 +395,7 @@
             barrier, inc=1, device_id={"src": lax.rem(s + d, n_src)}, device_id_type=MESH
         )
 
-    for load in small[:3]:
+    for load in small:
         load.wait()
     mine = jnp.int32(sn)
     shift = jnp.int32(0)
@@ -622,7 +620,6 @@
         inv_loads[k].wait()
         for d in range(1, n_src):
             inverse_copy(d, k).start()
-    small[3].wait()
     mask(0)
     mask(2)
     columns = [pl.ds(pl.multiple_of((k * n_blk + s) * BLK, BLK), BLK) for k in (0, 2)]
@@ -643,11 +640,11 @@
         running[c] = rhs[:, c * BLK : (c + 1) * BLK].astype(jnp.float32)
 
     relay(fac)
+    down_early(0)
     relay(0)
-    down_early(0)
-    down_early(fac)
     if chunks > 1:
         post_inner(1)
+    down_early(fac)
     down_late(fac)
     pick(fac)
     for q in range(2):
@@ -676,8 +673,8 @@
         elif c < chunks - 2:
             early(c)
     for c in range(chunks):
+        down_early(fac + 1 + c)
         relay(fac + 1 + c)
-        down_early(fac + 1 + c)
     gathered(1)
     for c in range(chunks):
         down_late(fac + 1 + c)
@@ -718,12 +715,9 @@
                     jax.ShapeDtypeStruct((kept, cols), jnp.bfloat16),
                     jax.ShapeDtypeStruct((rows, cols), jnp.bfloat16),
                 ),
-                in_specs=[hbm] * 6,
+                in_specs=[pl.BlockSpec(memory_space=pltpu.SMEM)] * 3 + [hbm] * 3,
                 out_specs=(vmem, vmem),
                 scratch_shapes=[
-                    pltpu.SMEM(pattern.shape, jnp.int32),
-                    pltpu.SMEM(owners.shape, jnp.int32),
-                    pltpu.SMEM(offsets.shape, jnp.int32),
                     pltpu.VMEM(right_side.shape, jnp.bfloat16),
                     pltpu.VMEM(factor.shape, jnp.bfloat16),
                     pltpu.VMEM((sn, n_src, inv_rows, snr), jnp.bfloat16),
@@ -737,7 +731,7 @@
                     pltpu.VMEM((2, *unit), jnp.bfloat16),
                     pltpu.VMEM((2, n_src, *unit), jnp.bfloat16),
                     pltpu.VMEM((2, snr, snr), jnp.bfloat16),
-                    pltpu.SemaphoreType.DMA((4,)),
+                    pltpu.SemaphoreType.DMA((1,)),
                     pltpu.SemaphoreType.DMA((sn,)),
                     pltpu.SemaphoreType.DMA((sn,)),
                     pltpu.SemaphoreType.DMA((sn, n_src)),
@@ -749,7 +743,7 @@
                     pltpu.SemaphoreType.DMA((units, 2, PIECES)),
                 ],
                 compiler_params=pltpu.CompilerParams(
-                    collective_id=0, has_side_effects=True, vmem_limit_bytes=63 * 1024 * 1024
+                    collective_id=0, has_side_effects=True, vmem_limit_bytes=53 * 1024 * 1024
                 ),
             )(pattern, owners, offsets, right_side, factor, inverses)
         return pl.pallas_call(

time: 66.6 us -> 58.5 us (0.88)
  Pallas kernels: 62.1 us -> 54.2 us
    pallas_call x1, Pallas kernels: 62.1 us -> 54.2 us  [on_device(): pl.pallas_call(functools.partial(pair_kernel, n_row, n_src), out_shape=(j...]
    unnamed x2 -> x8, local copies, waits for them, and re-layouts: 3.64 us -> 3.52 us
where the time goes in v2:
time: 58.5 us; the launch traced here: 58.4 us
  Pallas kernels  54.2 us (93%)
  local copies, waits for them, and re-layouts  3.52 us (6%)
  between operations  0.65 us (1%)
    pallas_call x1, Pallas kernels, on_device(): pl.pallas_call(functools.partial(pair_kernel, n_row, n_src), out_shape=(j...  54.2 us
    unnamed x8, local copies, waits for them, and re-layouts  3.52 us

profile of v2, /device:TPU:0, one launch (start us, length us, event | category | flops | bytes accessed | tf_op | source)
XLA Modules:
  0.0 58.4 jit_solution(11673957106751864485)
XLA Ops:
  0.6 0.0 copy-start
  0.6 0.7 %copy-done = s32[5,16]{1,0:T(8,128)S(1)} copy-done((s32[5,16]{1,0:T(8,128)S(1)}, s32[5,16]{1,0:T(8,128)}, u32[]{:S(2)}) %copy-start) | copy-done | bytes 344
  1.3 0.0 copy-start.1
  1.3 0.7 %copy-done.1 = s32[4]{0:T(128)S(1)} copy-done((s32[4]{0:T(128)S(1)}, s32[4]{0:T(128)}, u32[]{:S(2)}) %copy-start.1) | copy-done | bytes 40
  2.0 0.0 copy-start.2
  2.0 0.7 %copy-done.2 = s32[4]{0:T(128)S(1)} copy-done((s32[4]{0:T(128)S(1)}, s32[4]{0:T(128)}, u32[]{:S(2)}) %copy-start.2) | copy-done | bytes 40
  2.6 54.2 %shard_map.77 = (bf16[512,384]{1,0:T(8,128)(2,1)S(1)}, bf16[640,384]{1,0:T(8,128)(2,1)S(1)}) custom-call(s32[5,16]{1,0:T(8,128)S(1)} %copy-done, s32[4]{0:T(128)S(1)} %copy-done.1, s32[4]{0:T(128)S(1)} %copy-done.2, bf16[640,384]{1,0:T(8,128)(2,1)} %rhs_in.1, bf16[640,2048]{1,0:T(8,128)(2,1)} %factor.1, bf16[4,128,512]{2,1,0:T(8,128)(2,1)} %inverses_in.1), custom_call_target="tpu_custom_call" | custom-call | tf_op jit(solution)/shard_map/pallas_call | solution.py:712
  56.8 0.7 %copy.10 = bf16[512,384]{1,0:T(8,128)(2,1)} copy(bf16[512,384]{1,0:T(8,128)(2,1)S(1)} %get-tuple-element.4) | data formatting | bytes 786432
  57.6 0.8 %copy.11 = bf16[640,384]{1,0:T(8,128)(2,1)} copy(bf16[640,384]{1,0:T(8,128)(2,1)S(1)} %get-tuple-element.5) | data formatting | bytes 983040
Async XLA Ops:
  0.6 0.7 %copy-start = (s32[5,16]{1,0:T(8,128)S(1)}, s32[5,16]{1,0:T(8,128)}, u32[]{:S(2)}) copy-start(s32[5,16]{1,0:T(8,128)} %pattern.1) | copy-start | bytes 964
  1.3 0.7 %copy-start.1 = (s32[4]{0:T(128)S(1)}, s32[4]{0:T(128)}, u32[]{:S(2)}) copy-start(s32[4]{0:T(128)} %owners.1) | copy-start | bytes 52
  2.0 0.7 %copy-start.2 = (s32[4]{0:T(128)S(1)}, s32[4]{0:T(128)}, u32[]{:S(2)}) copy-start(s32[4]{0:T(128)} %offsets.1) | copy-start | bytes 52
